TPU v7x, 512 devices: a whole 4x8x8 slice. The times are simulated.
512 devices in a mesh: freq: 8 (over z), sx: 16 (over y, core), sy: 4 (over x).
Axes of the slice: x: 4, y: 8, z: 8, core: 2. Of those that a mesh axis runs over, the one named last changes fastest.
Arguments:
- stiffness: bfloat16 [16, 4, 3072, 3072], P('sx', 'sy', None, 'freq')
- mass_matrix: bfloat16 [16, 4, 3072, 3072], P('sx', 'sy', None, 'freq')
- omega_table: float32 [32], replicated, may hold values from 0.5 to 6
- assignment: int32 [32], P('freq'), may hold values from 0 to 31, each once
- adjoint_load: float32 [16, 4, 32, 2, 4, 768], P('sx', 'sy', 'freq'), as said below
- forward_state: bfloat16 [16, 4, 32, 2, 4, 768], P('sx', 'sy', 'freq'), may hold values from -6 to 6
- owner_index: int32 [16, 4, 4, 768], P('sx', 'sy'), may hold values from 0 to 1727
Outputs:
- adjoint: float32 [16, 4, 32, 2, 4, 768], P('sx', 'sy', 'freq')
- gradient: float32 [16, 4, 1728], P('sx', 'sy', 'freq')
- residual_level: float32 [32], P('freq')
Inputs may be any that keep to these rules, and one draw needn't show every extreme that they name: `adjoint_load`: the two copies of a face shared by neighbouring substructures are equal.
All inputs are finite; a program needn't handle non-finite values.
Results may differ from a plain program's by a relative error of at most 0.012.
Values may be sent and summed in bfloat16 or wider, within the bound.
No kernel may reach another device: no remote copies, remote signals or barrier semaphores. Data moves between devices by JAX's collectives and lax.ppermute only.
A program may use at most 64 MiB of HBM per device.

v0:
```python
import jax
import jax.numpy as jnp
from jax import lax
from jax.sharding import PartitionSpec as P

ITERS = 4
DE_SUB = 1728
LOSS_FACTOR = 0.3


def padded(cells, sides, width):
    for axis, dim in sides:
        count = lax.axis_size(axis)
        ends = count - 1
        head = lax.slice_in_dim(cells, 0, width, axis=dim)
        tail = lax.slice_in_dim(cells, cells.shape[dim] - width, cells.shape[dim], axis=dim)
        cells = jnp.concatenate(
            [
                lax.ppermute(tail, axis, [(i, (i + 1) % count) for i in range(ends)]),
                cells,
                lax.ppermute(head, axis, [((i + 1) % count, i) for i in range(ends)]),
            ],
            axis=dim,
        )
    return cells


def face_weights():
    index_x = lax.axis_index("sx")
    size_x = lax.axis_size("sx")
    index_y = lax.axis_index("sy")
    size_y = lax.axis_size("sy")
    west_weight = jnp.where(index_x > 0, 0.5, 1.0)
    east_weight = jnp.where(index_x < size_x - 1, 0.5, 1.0)
    south_weight = jnp.where(index_y > 0, 0.5, 1.0)
    north_weight = jnp.where(index_y < size_y - 1, 0.5, 1.0)
    return jnp.stack([west_weight, east_weight, south_weight, north_weight]).astype(jnp.float32)


def assemble(local_vals):
    padded_x = padded(local_vals[:, :, 0:2].astype(jnp.bfloat16), (("sx", 2),), 1).astype(
        jnp.float32
    )
    padded_y = padded(local_vals[:, :, 2:4].astype(jnp.bfloat16), (("sy", 2),), 1).astype(
        jnp.float32
    )
    west_face = padded_x[:, :, 1] + padded_x[:, :, 0]
    east_face = padded_x[:, :, 2] + padded_x[:, :, 3]
    south_face = padded_y[:, :, 1] + padded_y[:, :, 0]
    north_face = padded_y[:, :, 2] + padded_y[:, :, 3]
    return jnp.stack([west_face, east_face, south_face, north_face], axis=2)


def mix_parts(stiff_part, mass_part, omega_sq, sign_factor):
    factor = omega_sq[:, None, None]
    real_part = (
        stiff_part[:, 0] - sign_factor * LOSS_FACTOR * stiff_part[:, 1] - factor * mass_part[:, 0]
    )
    imag_part = (
        stiff_part[:, 1] + sign_factor * LOSS_FACTOR * stiff_part[:, 0] - factor * mass_part[:, 1]
    )
    return jnp.stack([real_part, imag_part], axis=1)


def apply_rows(vector, stiff_cols, mass_cols, omega_every, sign_factor):
    face_count = vector.shape[2]
    matrix_order = face_count * vector.shape[3]
    rounded = vector.astype(jnp.bfloat16)
    pieces = lax.all_gather(rounded, "freq", axis=0, tiled=True)
    count = pieces.shape[0]
    flattened = pieces.reshape(-1, matrix_order)
    stiff_part = jnp.dot(flattened, stiff_cols, preferred_element_type=jnp.float32)
    mass_part = jnp.dot(flattened, mass_cols, preferred_element_type=jnp.float32)
    local_vals = mix_parts(
        stiff_part.reshape(count, 2, face_count, -1),
        mass_part.reshape(count, 2, face_count, -1),
        omega_every,
        sign_factor,
    )
    returned = lax.all_to_all(
        local_vals.astype(jnp.bfloat16), "freq", split_axis=0, concat_axis=3, tiled=True
    ).astype(local_vals.dtype)
    return assemble(returned)


def reduce_dots(factor_pairs, weights):
    partial_value = tuple(
        (
            jnp.sum(first_vec * second_vec * weights[None, None, :, None], axis=(1, 2, 3))
            for first_vec, second_vec in factor_pairs
        )
    )
    summed = lax.psum(partial_value, ("sx", "sy"))
    return summed


def per_freq(values):
    return values[:, None, None, None]


def face_columns(matrix, matrix_order, face_count):
    grouped = matrix.reshape(matrix_order, -1, face_count)
    return jnp.swapaxes(grouped, 1, 2).reshape(matrix_order, -1)


def body(stiffness, mass_matrix, omega_table, assignment, adjoint_load, forward_state, owner_index):
    n_freq = lax.axis_size("freq")
    slot_count = adjoint_load.shape[2]
    face_count = adjoint_load.shape[4]
    face_len = adjoint_load.shape[5]
    matrix_order = face_count * face_len
    stiff_cols = face_columns(stiffness[0, 0], matrix_order, face_count)
    mass_cols = face_columns(mass_matrix[0, 0], matrix_order, face_count)
    matches = assignment[:, None] == jnp.arange(omega_table.shape[0], dtype=jnp.int32)[None, :]
    slot_omega = jnp.sum(jnp.where(matches, omega_table[None, :], 0.0), axis=1)
    weights = face_weights()
    load_rows = adjoint_load[0, 0]
    omega_every = lax.all_gather(slot_omega, "freq", axis=0, tiled=True)

    def operate(vector, sign_factor):
        return apply_rows(vector, stiff_cols, mass_cols, omega_every, sign_factor)

    residual = load_rows
    solution = jnp.zeros_like(load_rows)
    normal_res = operate(residual, -1.0)
    direction = normal_res
    gamma_now = reduce_dots(((normal_res, normal_res),), weights)[0]
    for iteration in range(ITERS):
        image_vec = operate(direction, 1.0)
        delta_now = reduce_dots(((image_vec, image_vec),), weights)[0]
        step_size = gamma_now / delta_now
        solution = solution + per_freq(step_size) * direction
        if iteration + 1 < ITERS:
            residual = residual - per_freq(step_size) * image_vec
            normal_res = operate(residual, -1.0)
            gamma_next = reduce_dots(((normal_res, normal_res),), weights)[0]
            direction = normal_res + per_freq(gamma_next / gamma_now) * direction
            gamma_now = gamma_next
    cell_count = float(lax.axis_size("sx") * lax.axis_size("sy") * 2 * matrix_order)
    residual_level = jnp.log(gamma_now / cell_count)
    state_vec = forward_state[0, 0].astype(jnp.float32)
    lambda_real = solution[:, 0]
    lambda_imag = solution[:, 1]
    state_real = state_vec[:, 0]
    state_imag = state_vec[:, 1]
    product_term = (
        lambda_real * state_real
        - lambda_imag * state_imag
        - LOSS_FACTOR * (lambda_real * state_imag + lambda_imag * state_real)
    )
    dof_total = jnp.sum(product_term, axis=0)
    partial_grad = jax.ops.segment_sum(
        dof_total.reshape(-1), owner_index[0, 0].reshape(-1), num_segments=DE_SUB
    )
    grad_factor = (DE_SUB / (slot_count * n_freq * matrix_order)) ** 0.5
    gradient = lax.psum_scatter(
        -grad_factor * partial_grad, "freq", scatter_dimension=0, tiled=True
    )
    return (solution[None, None], gradient[None, None], residual_level)


def solution(mesh):
    return jax.shard_map(
        body,
        mesh=mesh,
        in_specs=(
            P("sx", "sy", None, "freq"),
            P("sx", "sy", None, "freq"),
            P(),
            P("freq"),
            P("sx", "sy", "freq", None, None, None),
            P("sx", "sy", "freq", None, None, None),
            P("sx", "sy", None, None),
        ),
        out_specs=(P("sx", "sy", "freq", None, None, None), P("sx", "sy", "freq"), P("freq")),
        check_vma=False,
    )
```

profile of v0, /device:TPU:32, one launch (start us, length us, event | category | flops | bytes accessed | tf_op | source)
XLA Modules:
  0.0 1387.7 jit_solution(9510212069884050593)
XLA Ops:
  0.6 2.8 copy.77
  3.5 2.3 reshape_squeeze.7
  5.9 31.4 %all_gather.27 = bf16[32,2,4,768]{3,2,1,0:T(4,128)(2,1)S(1)} all-gather(bf16[4,2,4,768]{3,2,1,0:T(4,128)(2,1)S(1)} %bitcast_convert_fusion), channel_id=1, replica_groups=mesh['freq'=8,'sx'=16,'sy'=4] {'freq'}, dimensions={0}, use_global_device_ids=true | all-gather | bytes 442368 | tf_op jit(solution)/shard_map/all_gather | solution.py:69
  37.4 2.8 copy.75
  40.2 2.4 reshape_squeeze.6
  42.6 2.9 fusion.14
  48.3 17.0 %all-reduce = f32[32]{0:T(128)S(1)} all-reduce(f32[32]{0:T(128)S(1)} %dynamic-update-slice), channel_id=1, replica_groups=mesh['freq'=8,'sx'=16,'sy'=4] {'freq'}, use_global_device_ids=true, to_apply=%add | all-reduce | flops 32 | bytes 256
  66.1 3.4 all-to-all-start
  69.5 8.3 all-to-all-done
  78.0 1.9 collective-permute-start.1
  80.0 2.4 collective-permute-start
  83.7 4.5 collective-permute-start.2
  90.1 25.1 %all_gather.29 = bf16[32,2,4,768]{3,2,1,0:T(4,128)(2,1)S(1)} all-gather(bf16[4,2,4,768]{3,2,1,0:T(4,128)(2,1)S(1)} %fusion.103), channel_id=1, replica_groups=mesh['freq'=8,'sx'=16,'sy'=4] {'freq'}, dimensions={0}, use_global_device_ids=true | all-gather | bytes 442368 | tf_op jit(solution)/shard_map/all_gather | solution.py:69
  118.9 3.4 all-to-all-start.1
  122.3 8.2 all-to-all-done.1
  132.1 5.0 collective-permute-start.6
  137.1 1.9 collective-permute-start.5
  139.0 2.4 collective-permute-start.4
  141.6 3.8 collective-permute-done.4
  145.9 126.0 %all-reduce.2 = (f32[4]{0:T(128)S(1)}, f32[4]{0:T(128)S(1)}) all-reduce(f32[4]{0:T(128)S(1)} %get-tuple-element.4, f32[4]{0:T(128)S(1)} %get-tuple-element.3), channel_id=1, replica_groups=mesh['freq'=8,'sx'=16,'sy'=4] {'sx','sy'}, use_global_device_ids=true, to_apply=%region_2.3 | all-reduce | flops 8 | bytes 64 | tf_op jit(solution)/shard_map/psum | solution.py:93
  272.1 25.5 %all_gather.30 = bf16[32,2,4,768]{3,2,1,0:T(4,128)(2,1)S(1)} all-gather(bf16[4,2,4,768]{3,2,1,0:T(4,128)(2,1)S(1)} %get-tuple-element.13), channel_id=1, replica_groups=mesh['freq'=8,'sx'=16,'sy'=4] {'freq'}, dimensions={0}, use_global_device_ids=true | all-gather | bytes 442368 | tf_op jit(solution)/shard_map/all_gather | solution.py:69
  300.6 10.8 all_to_all.32
  312.9 4.5 collective-permute-start.10
  317.5 1.9 collective-permute-start.9
  319.4 2.4 collective-permute-start.8
  322.0 3.7 collective-permute-done.8
  326.2 124.5 %psum.58 = f32[4]{0:T(128)S(1)} all-reduce(f32[4]{0:T(128)S(1)} %multiply_reduce_fusion.4), channel_id=1, replica_groups=mesh['freq'=8,'sx'=16,'sy'=4] {'sx','sy'}, use_global_device_ids=true, to_apply=%region_6.7 | all-reduce | flops 4 | bytes 32 | tf_op jit(solution)/shard_map/psum | solution.py:93
  450.9 25.0 %all_gather.31 = bf16[32,2,4,768]{3,2,1,0:T(4,128)(2,1)S(1)} all-gather(bf16[4,2,4,768]{3,2,1,0:T(4,128)(2,1)S(1)} %get-tuple-element.11), channel_id=1, replica_groups=mesh['freq'=8,'sx'=16,'sy'=4] {'freq'}, dimensions={0}, use_global_device_ids=true | all-gather | bytes 442368 | tf_op jit(solution)/shard_map/all_gather | solution.py:69
  479.0 11.0 all_to_all.33
  491.6 5.1 collective-permute-start.14
  496.7 1.9 collective-permute-start.13
  498.6 2.4 collective-permute-start.12
  501.2 3.8 collective-permute-done.12
  505.4 126.1 %psum.59 = f32[4]{0:T(128)S(1)} all-reduce(f32[4]{0:T(128)S(1)} %multiply_reduce_fusion.3), channel_id=1, replica_groups=mesh['freq'=8,'sx'=16,'sy'=4] {'sx','sy'}, use_global_device_ids=true, to_apply=%region_8.9 | all-reduce | flops 4 | bytes 32 | tf_op jit(solution)/shard_map/psum | solution.py:93
  632.2 25.5 %all_gather.32 = bf16[32,2,4,768]{3,2,1,0:T(4,128)(2,1)S(1)} all-gather(bf16[4,2,4,768]{3,2,1,0:T(4,128)(2,1)S(1)} %get-tuple-element.9), channel_id=1, replica_groups=mesh['freq'=8,'sx'=16,'sy'=4] {'freq'}, dimensions={0}, use_global_device_ids=true | all-gather | bytes 442368 | tf_op jit(solution)/shard_map/all_gather | solution.py:69
  660.7 10.8 all_to_all.34
  673.0 4.5 collective-permute-start.18
  677.6 1.9 collective-permute-start.17
  679.6 2.4 collective-permute-start.16
  682.2 3.7 collective-permute-done.16
  686.3 124.3 %psum.60 = f32[4]{0:T(128)S(1)} all-reduce(f32[4]{0:T(128)S(1)} %multiply_reduce_fusion.2), channel_id=1, replica_groups=mesh['freq'=8,'sx'=16,'sy'=4] {'sx','sy'}, use_global_device_ids=true, to_apply=%region_10.11 | all-reduce | flops 4 | bytes 32 | tf_op jit(solution)/shard_map/psum | solution.py:93
  811.1 25.0 %all_gather.33 = bf16[32,2,4,768]{3,2,1,0:T(4,128)(2,1)S(1)} all-gather(bf16[4,2,4,768]{3,2,1,0:T(4,128)(2,1)S(1)} %get-tuple-element.7), channel_id=1, replica_groups=mesh['freq'=8,'sx'=16,'sy'=4] {'freq'}, dimensions={0}, use_global_device_ids=true | all-gather | bytes 442368 | tf_op jit(solution)/shard_map/all_gather | solution.py:69
  839.2 11.0 all_to_all.35
  851.8 4.8 collective-permute-start.22
  856.6 1.9 collective-permute-start.21
  858.6 2.4 collective-permute-start.20
  861.2 3.8 collective-permute-done.20
  865.3 126.1 %psum.61 = f32[4]{0:T(128)S(1)} all-reduce(f32[4]{0:T(128)S(1)} %multiply_reduce_fusion.1), channel_id=1, replica_groups=mesh['freq'=8,'sx'=16,'sy'=4] {'sx','sy'}, use_global_device_ids=true, to_apply=%region_12.13 | all-reduce | flops 4 | bytes 32 | tf_op jit(solution)/shard_map/psum | solution.py:93
  992.0 25.7 %all_gather.34 = bf16[32,2,4,768]{3,2,1,0:T(4,128)(2,1)S(1)} all-gather(bf16[4,2,4,768]{3,2,1,0:T(4,128)(2,1)S(1)} %subtract_convert_fusion), channel_id=1, replica_groups=mesh['freq'=8,'sx'=16,'sy'=4] {'freq'}, dimensions={0}, use_global_device_ids=true | all-gather | bytes 442368 | tf_op jit(solution)/shard_map/all_gather | solution.py:69
  1020.7 10.8 all_to_all.36
  1033.0 4.5 collective-permute-start.26
  1037.6 1.9 collective-permute-start.25
  1039.6 2.4 collective-permute-start.24
  1042.2 3.8 collective-permute-done.24
  1046.3 124.3 %psum.62 = f32[4]{0:T(128)S(1)} all-reduce(f32[4]{0:T(128)S(1)} %multiply_reduce_fusion), channel_id=1, replica_groups=mesh['freq'=8,'sx'=16,'sy'=4] {'sx','sy'}, use_global_device_ids=true, to_apply=%region_14.15 | all-reduce | flops 4 | bytes 32 | tf_op jit(solution)/shard_map/psum | solution.py:93
  1171.2 25.0 %all_gather.35 = bf16[32,2,4,768]{3,2,1,0:T(4,128)(2,1)S(1)} all-gather(bf16[4,2,4,768]{3,2,1,0:T(4,128)(2,1)S(1)} %fusion.68), channel_id=1, replica_groups=mesh['freq'=8,'sx'=16,'sy'=4] {'freq'}, dimensions={0}, use_global_device_ids=true | all-gather | bytes 442368 | tf_op jit(solution)/shard_map/all_gather | solution.py:69
  1200.0 3.4 all-to-all-start.7
  1203.5 8.2 all-to-all-done.7
  1213.2 4.7 collective-permute-start.30
  1219.9 2.4 collective-permute-start.28
  1222.5 3.8 collective-permute-done.28
  1227.3 126.1 %psum.63 = f32[4]{0:T(128)S(1)} all-reduce(f32[4]{0:T(128)S(1)} %fusion.65), channel_id=1, replica_groups=mesh['freq'=8,'sx'=16,'sy'=4] {'sx','sy'}, use_global_device_ids=true, to_apply=%region_16.17 | all-reduce | flops 4 | bytes 32 | tf_op jit(solution)/shard_map/psum | solution.py:93
  1354.2 16.8 %scatter_custom_fusion = f32[1728]{0:T(1024)S(1)} fusion(s32[3072]{0:T(1024)S(1)} %reshape.442, f32[3072]{0:T(1024)S(1)} %reshape.444, f32[]{:T(128)} %constant.14.clone.1), kind=kCustom, calls=%fused_computation.212 | custom fusion | flops 3072 | bytes 6916 | tf_op jit(solution)/shard_map/scatter-add | solution.py:152
  1371.0 15.0 %all-reduce.1 = f32[1728]{0:T(1024)S(1)} all-reduce(f32[1728]{0:T(1024)S(1)} %broadcast_multiply_fusion), channel_id=2, replica_groups=mesh['freq'=8,'sx'=16,'sy'=4] {'freq'}, use_global_device_ids=true, to_apply=%region_19.20.clone | all-reduce | flops 1728 | bytes 13824
  (271 shorter events, 50.8 us)
Async XLA Ops:
  46.6 68.7 %copy-start = (bf16[3072,96,4]{0,2,1:T(4,128)(2,1)S(1)}, bf16[3072,96,4]{0,2,1:T(4,128)(2,1)}, u32[]{:S(2)}) copy-start(bf16[3072,96,4]{0,2,1:T(4,128)(2,1)} %reshape_squeeze.7) | copy-start | bytes 7077892
  66.1 11.7 all-to-all-start
  78.0 10.2 collective-permute-start.1
  80.0 8.3 collective-permute-start
  82.4 5.9 collective-permute-start.3
  83.7 6.1 collective-permute-start.2
  118.9 11.7 all-to-all-start.1
  130.8 10.7 collective-permute-start.7
  132.1 9.4 collective-permute-start.6
  137.1 4.5 collective-permute-start.5
  139.0 6.4 collective-permute-start.4
  311.6 10.2 collective-permute-start.11
  312.9 9.0 collective-permute-start.10
  317.5 4.5 collective-permute-start.9
  319.4 6.4 collective-permute-start.8
  322.0 128.8 %copy-start.9 = (f32[4,2,1,768]{3,2,1,0:T(1,128)}, f32[4,2,1,768]{3,2,1,0:T(1,128)S(1)}, u32[]{:S(2)}) copy-start(f32[4,2,1,768]{3,2,1,0:T(1,128)S(1)} %get-tuple-element.53) | copy-start | bytes 73732
  322.0 128.8 %copy-start.11 = (f32[4,2,1,768]{3,2,1,0:T(1,128)}, f32[4,2,1,768]{3,2,1,0:T(1,128)S(1)}, u32[]{:S(2)}) copy-start(f32[4,2,1,768]{3,2,1,0:T(1,128)S(1)} %get-tuple-element.54) | copy-start | bytes 73732
  325.9 124.9 %copy-start.13 = (f32[4,2,1,768]{3,2,1,0:T(1,128)}, f32[4,2,1,768]{3,2,1,0:T(1,128)S(1)}, u32[]{:S(2)}) copy-start(f32[4,2,1,768]{3,2,1,0:T(1,128)S(1)} %get-tuple-element.51) | copy-start | bytes 73732
  325.9 124.9 %copy-start.15 = (f32[4,2,1,768]{3,2,1,0:T(1,128)}, f32[4,2,1,768]{3,2,1,0:T(1,128)S(1)}, u32[]{:S(2)}) copy-start(f32[4,2,1,768]{3,2,1,0:T(1,128)S(1)} %get-tuple-element.52) | copy-start | bytes 73732
  450.6 39.4 %copy-start.41 = (f32[4]{0:T(128)}, f32[4]{0:T(128)S(1)}, u32[]{:S(2)}) copy-start(f32[4]{0:T(128)S(1)} %psum.58) | copy-start | bytes 52
  450.6 26.5 %copy-start.32 = (f32[4]{0:T(128)}, f32[4]{0:T(128)S(1)}, u32[]{:S(2)}) copy-start(f32[4]{0:T(128)S(1)} %div.25) | copy-start | bytes 52
  490.3 10.8 collective-permute-start.15
  491.6 9.5 collective-permute-start.14
  496.7 4.5 collective-permute-start.13
  498.6 6.4 collective-permute-start.12
  659.5 151.1 %copy-start.42 = (f32[4]{0:T(128)S(1)}, f32[4]{0:T(128)}, u32[]{:S(2)}) copy-start(f32[4]{0:T(128)} %copy-done.41) | copy-start | bytes 52
  671.7 10.2 collective-permute-start.19
  673.0 9.0 collective-permute-start.18
  677.6 4.5 collective-permute-start.17
  679.6 6.4 collective-permute-start.16
  682.1 128.6 %copy-start.17 = (f32[4,2,1,768]{3,2,1,0:T(1,128)}, f32[4,2,1,768]{3,2,1,0:T(1,128)S(1)}, u32[]{:S(2)}) copy-start(f32[4,2,1,768]{3,2,1,0:T(1,128)S(1)} %get-tuple-element.45) | copy-start | bytes 73732
  682.2 128.6 %copy-start.19 = (f32[4,2,1,768]{3,2,1,0:T(1,128)}, f32[4,2,1,768]{3,2,1,0:T(1,128)S(1)}, u32[]{:S(2)}) copy-start(f32[4,2,1,768]{3,2,1,0:T(1,128)S(1)} %get-tuple-element.46) | copy-start | bytes 73732
  686.1 124.7 %copy-start.21 = (f32[4,2,1,768]{3,2,1,0:T(1,128)}, f32[4,2,1,768]{3,2,1,0:T(1,128)S(1)}, u32[]{:S(2)}) copy-start(f32[4,2,1,768]{3,2,1,0:T(1,128)S(1)} %get-tuple-element.43) | copy-start | bytes 73732
  686.1 124.7 %copy-start.23 = (f32[4,2,1,768]{3,2,1,0:T(1,128)}, f32[4,2,1,768]{3,2,1,0:T(1,128)S(1)}, u32[]{:S(2)}) copy-start(f32[4,2,1,768]{3,2,1,0:T(1,128)S(1)} %get-tuple-element.44) | copy-start | bytes 73732
  838.0 153.4 %copy-start.44 = (f32[4]{0:T(128)S(1)}, f32[4]{0:T(128)}, u32[]{:S(2)}) copy-start(f32[4]{0:T(128)} %copy-done.43) | copy-start | bytes 52
  850.5 10.5 collective-permute-start.23
  851.8 9.2 collective-permute-start.22
  856.6 4.5 collective-permute-start.21
  858.6 6.4 collective-permute-start.20
  1019.5 151.1 %copy-start.45 = (f32[4]{0:T(128)S(1)}, f32[4]{0:T(128)}, u32[]{:S(2)}) copy-start(f32[4]{0:T(128)} %copy-done.43) | copy-start | bytes 52
  1031.7 10.2 collective-permute-start.27
  1033.0 9.0 collective-permute-start.26
  1037.6 4.5 collective-permute-start.25
  1039.6 6.4 collective-permute-start.24
  1198.1 5.4 copy-start.26
  1198.1 5.4 copy-start.27
  1198.1 155.3 %copy-start.38 = (f32[4]{0:T(128)S(1)}, f32[4]{0:T(128)}, u32[]{:S(2)}) copy-start(f32[4]{0:T(128)} %copy-done.37) | copy-start | bytes 52
  1198.1 155.8 %copy-start.29 = (f32[4]{0:T(128)S(1)}, f32[4]{0:T(128)}, u32[]{:S(2)}) copy-start(f32[4]{0:T(128)} %copy-done.28) | copy-start | bytes 52
  1198.1 155.8 %copy-start.31 = (f32[4]{0:T(128)S(1)}, f32[4]{0:T(128)}, u32[]{:S(2)}) copy-start(f32[4]{0:T(128)} %copy-done.30) | copy-start | bytes 52
  1199.2 187.4 %copy-start.10 = (f32[4,2,1,768]{3,2,1,0:T(1,128)S(1)}, f32[4,2,1,768]{3,2,1,0:T(1,128)}, u32[]{:S(2)}) copy-start(f32[4,2,1,768]{3,2,1,0:T(1,128)} %copy-done.9) | copy-start | bytes 73732
  1199.2 187.4 %copy-start.12 = (f32[4,2,1,768]{3,2,1,0:T(1,128)S(1)}, f32[4,2,1,768]{3,2,1,0:T(1,128)}, u32[]{:S(2)}) copy-start(f32[4,2,1,768]{3,2,1,0:T(1,128)} %copy-done.11) | copy-start | bytes 73732
  1199.2 187.4 %copy-start.14 = (f32[4,2,1,768]{3,2,1,0:T(1,128)S(1)}, f32[4,2,1,768]{3,2,1,0:T(1,128)}, u32[]{:S(2)}) copy-start(f32[4,2,1,768]{3,2,1,0:T(1,128)} %copy-done.13) | copy-start | bytes 73732
  1199.2 187.4 %copy-start.16 = (f32[4,2,1,768]{3,2,1,0:T(1,128)S(1)}, f32[4,2,1,768]{3,2,1,0:T(1,128)}, u32[]{:S(2)}) copy-start(f32[4,2,1,768]{3,2,1,0:T(1,128)} %copy-done.15) | copy-start | bytes 73732
  1199.2 187.4 %copy-start.18 = (f32[4,2,1,768]{3,2,1,0:T(1,128)S(1)}, f32[4,2,1,768]{3,2,1,0:T(1,128)}, u32[]{:S(2)}) copy-start(f32[4,2,1,768]{3,2,1,0:T(1,128)} %copy-done.17) | copy-start | bytes 73732
  1199.2 187.4 %copy-start.20 = (f32[4,2,1,768]{3,2,1,0:T(1,128)S(1)}, f32[4,2,1,768]{3,2,1,0:T(1,128)}, u32[]{:S(2)}) copy-start(f32[4,2,1,768]{3,2,1,0:T(1,128)} %copy-done.19) | copy-start | bytes 73732
  1199.2 187.4 %copy-start.22 = (f32[4,2,1,768]{3,2,1,0:T(1,128)S(1)}, f32[4,2,1,768]{3,2,1,0:T(1,128)}, u32[]{:S(2)}) copy-start(f32[4,2,1,768]{3,2,1,0:T(1,128)} %copy-done.21) | copy-start | bytes 73732
  1199.2 187.4 %copy-start.24 = (f32[4,2,1,768]{3,2,1,0:T(1,128)S(1)}, f32[4,2,1,768]{3,2,1,0:T(1,128)}, u32[]{:S(2)}) copy-start(f32[4,2,1,768]{3,2,1,0:T(1,128)} %copy-done.23) | copy-start | bytes 73732
  1199.2 187.4 %copy-start.33 = (f32[4]{0:T(128)S(1)}, f32[4]{0:T(128)}, u32[]{:S(2)}) copy-start(f32[4]{0:T(128)} %copy-done.32) | copy-start | bytes 52
  1199.3 187.4 %copy-start.35 = (f32[4]{0:T(128)S(1)}, f32[4]{0:T(128)}, u32[]{:S(2)}) copy-start(f32[4]{0:T(128)} %copy-done.34) | copy-start | bytes 52
  1200.0 11.7 all-to-all-start.7
  1211.9 10.4 collective-permute-start.31
  1213.2 9.1 collective-permute-start.30
  1218.0 4.5 collective-permute-start.29
  1219.9 6.4 collective-permute-start.28
  (17 other events, 23.1 us)
where the time goes:
time: 1390 us
  blocking collectives  1170 us (84%)
  starting transfers between devices  92.8 us (7%)
  waiting for transfers between devices  52.5 us (4%)
  other arithmetic  25.2 us (2%)
  local copies, waits for them, and re-layouts  23 us (2%)
  matrix products  18.9 us (1%)
    psum x7, blocking collectives, reduce_dots(): summed = lax.psum(partial_value, ('sx', 'sy'))  877 us
    all_gather x8, blocking collectives, apply_rows(): pieces = lax.all_gather(rounded, 'freq', axis=0, tiled=True)  208 us
    ppermute x16, starting transfers between devices, padded(): lax.ppermute(tail, axis, [(i, (i + 1) % count) for i in range(ends)])  57 us
    all_to_all x5, blocking collectives, apply_rows(): lax.all_to_all(local_vals.astype(jnp.bfloat16), 'freq', split_axis=0, con...  54.3 us
    unnamed x2, blocking collectives  32 us
  transfers between devices with their start and end apart: 35, of which 11 were waited for; matrix products, arithmetic and copies ran while one was open for 0% of the time, Pallas kernels for 0%

commit v1 on v0

--- a/solution.py
+++ b/solution.py
@@ -1,3 +1,4 @@
+import functools
 import jax
 import jax.numpy as jnp
 from jax import lax
@@ -6,6 +7,14 @@
 ITERS = 4
 DE_SUB = 1728
 LOSS_FACTOR = 0.3
+
+
+def test_boxes(in_array, lane_axis, dev_axis):
+    taken_in = lax.psum(in_array, dev_axis)
+    return lax.psum(taken_in, lane_axis)
+
+
+fit_steps_all = functools.partial(test_boxes, lane_axis="sx", dev_axis="sy")
 
 
 def padded(cells, sides, width):
@@ -90,7 +99,7 @@
             for first_vec, second_vec in factor_pairs
         )
     )
-    summed = lax.psum(partial_value, ("sx", "sy"))
+    summed = fit_steps_all(partial_value)
     return summed
 
 

time: 1390 us -> 738 us (0.53)
  blocking collectives: 1170 us -> 521 us
    psum x7 -> x14, blocking collectives: 877 us -> 227 us  [the longest x7 165 us: test_boxes(): return lax.psum(taken_in, lane_axis)]
where the time goes in v1:
time: 738 us; the launch traced here: 736 us
  blocking collectives  521 us (71%)
  starting transfers between devices  91.8 us (12%)
  waiting for transfers between devices  52.5 us (7%)
  other arithmetic  25.2 us (3%)
  local copies, waits for them, and re-layouts  23 us (3%)
  matrix products  18.9 us (3%)
    all_gather x8, blocking collectives, apply_rows(): pieces = lax.all_gather(rounded, 'freq', axis=0, tiled=True)  208 us
    psum x7, blocking collectives, test_boxes(): return lax.psum(taken_in, lane_axis)  165 us
    psum x7, blocking collectives, test_boxes(): taken_in = lax.psum(in_array, dev_axis)  62.3 us
    ppermute x16, starting transfers between devices, padded(): lax.ppermute(tail, axis, [(i, (i + 1) % count) for i in range(ends)])  56.1 us
    all_to_all x5, blocking collectives, apply_rows(): lax.all_to_all(local_vals.astype(jnp.bfloat16), 'freq', split_axis=0, con...  54.6 us
    unnamed x2, blocking collectives  32 us
    ppermute x16, waiting for transfers between devices, padded(): lax.ppermute(tail, axis, [(i, (i + 1) % count) for i in range(ends)])  27.7 us
    ppermute x16, starting transfers between devices, padded(): lax.ppermute(head, axis, [((i + 1) % count, i) for i in range(ends)])  25.7 us
  transfers between devices with their start and end apart: 35, of which 11 were waited for; matrix products, arithmetic and copies ran while one was open for 0% of the time, Pallas kernels for 0%

profile of v1, /device:TPU:32, one launch (start us, length us, event | category | flops | bytes accessed | tf_op | source)
XLA Modules:
  0.0 736.2 jit_solution(10709400802163857110)
XLA Ops:
  0.6 2.8 copy.77
  3.5 2.3 reshape_squeeze.7
  5.8 31.4 %all_gather.27 = bf16[32,2,4,768]{3,2,1,0:T(4,128)(2,1)S(1)} all-gather(bf16[4,2,4,768]{3,2,1,0:T(4,128)(2,1)S(1)} %bitcast_convert_fusion), channel_id=1, replica_groups=mesh['freq'=8,'sx'=16,'sy'=4] {'freq'}, dimensions={0}, use_global_device_ids=true | all-gather | bytes 442368 | tf_op jit(solution)/shard_map/all_gather | solution.py:78
  37.4 2.8 copy.75
  40.2 2.3 reshape_squeeze.6
  42.5 2.9 fusion.14
  48.3 17.0 %all-reduce = f32[32]{0:T(128)S(1)} all-reduce(f32[32]{0:T(128)S(1)} %dynamic-update-slice), channel_id=1, replica_groups=mesh['freq'=8,'sx'=16,'sy'=4] {'freq'}, use_global_device_ids=true, to_apply=%add | all-reduce | flops 32 | bytes 256
  66.1 3.4 all-to-all-start
  69.5 8.3 %all-to-all-done = bf16[32,2,4,96]{3,2,1,0:T(4,128)(2,1)S(1)} async-done(((bf16[32,2,4,96]{3,2,1,0:T(4,128)(2,1)}), bf16[32,2,4,96]{3,2,1,0:T(4,128)(2,1)S(1)}, u32[]{:S(2)}, u32[]{:S(2)}) %all-to-all-start) | async-done | bytes 49184 | tf_op jit(solution)/shard_map/all_to_all | solution.py:89
  79.9 2.4 collective-permute-start
  83.6 4.5 collective-permute-start.2
  90.1 25.1 %all_gather.29 = bf16[32,2,4,768]{3,2,1,0:T(4,128)(2,1)S(1)} all-gather(bf16[4,2,4,768]{3,2,1,0:T(4,128)(2,1)S(1)} %fusion.103), channel_id=1, replica_groups=mesh['freq'=8,'sx'=16,'sy'=4] {'freq'}, dimensions={0}, use_global_device_ids=true | all-gather | bytes 442368 | tf_op jit(solution)/shard_map/all_gather | solution.py:78
  118.8 3.4 all-to-all-start.1
  122.3 8.2 %all-to-all-done.1 = bf16[32,2,4,96]{3,2,1,0:T(4,128)(2,1)S(1)} async-done(((bf16[32,2,4,96]{3,2,1,0:T(4,128)(2,1)}), bf16[32,2,4,96]{3,2,1,0:T(4,128)(2,1)S(1)}, u32[]{:S(2)}, u32[]{:S(2)}) %all-to-all-start.1) | async-done | bytes 49184 | tf_op jit(solution)/shard_map/all_to_all | solution.py:89
  132.0 5.0 collective-permute-start.6
  139.0 2.4 collective-permute-start.4
  141.6 3.8 collective-permute-done.4
  145.8 9.7 %all-reduce.3 = (f32[4]{0:T(128)S(1)}, f32[4]{0:T(128)S(1)}) all-reduce(f32[4]{0:T(128)S(1)} %get-tuple-element.4, f32[4]{0:T(128)S(1)} %get-tuple-element.3), channel_id=1, replica_groups=mesh['freq'=8,'sx'=16,'sy'=4] {'sy'}, use_global_device_ids=true, to_apply=%region_2.3 | all-reduce | flops 8 | bytes 64 | tf_op jit(solution)/shard_map/psum | solution.py:13
  155.6 23.5 %all-reduce.2 = (f32[4]{0:T(128)S(1)}, f32[4]{0:T(128)S(1)}) all-reduce(f32[4]{0:T(128)S(1)} %get-tuple-element.7, f32[4]{0:T(128)S(1)} %get-tuple-element.8), channel_id=1, replica_groups=mesh['freq'=8,'sx'=16,'sy'=4] {'sx'}, use_global_device_ids=true, to_apply=%region_3.4 | all-reduce | flops 8 | bytes 64 | tf_op jit(solution)/shard_map/psum | solution.py:14
  179.2 25.2 %all_gather.30 = bf16[32,2,4,768]{3,2,1,0:T(4,128)(2,1)S(1)} all-gather(bf16[4,2,4,768]{3,2,1,0:T(4,128)(2,1)S(1)} %get-tuple-element.15), channel_id=1, replica_groups=mesh['freq'=8,'sx'=16,'sy'=4] {'freq'}, dimensions={0}, use_global_device_ids=true | all-gather | bytes 442368 | tf_op jit(solution)/shard_map/all_gather | solution.py:78
  207.5 10.9 %all_to_all.32 = bf16[32,2,4,96]{3,2,1,0:T(4,128)(2,1)S(1)} all-to-all(bf16[32,2,4,96]{3,2,1,0:T(4,128)(2,1)S(1)} %copy.85), channel_id=1, replica_groups=mesh['freq'=8,'sx'=16,'sy'=4] {'freq'}, dimensions={0} | all-to-all | bytes 98304 | tf_op jit(solution)/shard_map/all_to_all | solution.py:89
  219.9 4.5 collective-permute-start.10
  226.4 2.4 collective-permute-start.8
  229.1 3.7 collective-permute-done.8
  233.2 8.8 %psum.116 = f32[4]{0:T(128)S(1)} all-reduce(f32[4]{0:T(128)S(1)} %multiply_reduce_fusion.4), channel_id=1, replica_groups=mesh['freq'=8,'sx'=16,'sy'=4] {'sy'}, use_global_device_ids=true, to_apply=%region_8.9 | all-reduce | flops 4 | bytes 32 | tf_op jit(solution)/shard_map/psum | solution.py:13
  241.9 23.5 %psum.117 = f32[4]{0:T(128)S(1)} all-reduce(f32[4]{0:T(128)S(1)} %psum.116), channel_id=1, replica_groups=mesh['freq'=8,'sx'=16,'sy'=4] {'sx'}, use_global_device_ids=true, to_apply=%region_9.10 | all-reduce | flops 4 | bytes 32 | tf_op jit(solution)/shard_map/psum | solution.py:14
  265.7 25.2 %all_gather.31 = bf16[32,2,4,768]{3,2,1,0:T(4,128)(2,1)S(1)} all-gather(bf16[4,2,4,768]{3,2,1,0:T(4,128)(2,1)S(1)} %get-tuple-element.13), channel_id=1, replica_groups=mesh['freq'=8,'sx'=16,'sy'=4] {'freq'}, dimensions={0}, use_global_device_ids=true | all-gather | bytes 442368 | tf_op jit(solution)/shard_map/all_gather | solution.py:78
  294.0 10.9 %all_to_all.33 = bf16[32,2,4,96]{3,2,1,0:T(4,128)(2,1)S(1)} all-to-all(bf16[32,2,4,96]{3,2,1,0:T(4,128)(2,1)S(1)} %copy.88), channel_id=1, replica_groups=mesh['freq'=8,'sx'=16,'sy'=4] {'freq'}, dimensions={0} | all-to-all | bytes 98304 | tf_op jit(solution)/shard_map/all_to_all | solution.py:89
  306.4 4.5 collective-permute-start.14
  312.9 2.4 collective-permute-start.12
  315.6 3.8 collective-permute-done.12
  319.7 8.9 %psum.118 = f32[4]{0:T(128)S(1)} all-reduce(f32[4]{0:T(128)S(1)} %multiply_reduce_fusion.3), channel_id=1, replica_groups=mesh['freq'=8,'sx'=16,'sy'=4] {'sy'}, use_global_device_ids=true, to_apply=%region_11.12 | all-reduce | flops 4 | bytes 32 | tf_op jit(solution)/shard_map/psum | solution.py:13
  328.5 23.5 %psum.119 = f32[4]{0:T(128)S(1)} all-reduce(f32[4]{0:T(128)S(1)} %psum.118), channel_id=1, replica_groups=mesh['freq'=8,'sx'=16,'sy'=4] {'sx'}, use_global_device_ids=true, to_apply=%region_12.13 | all-reduce | flops 4 | bytes 32 | tf_op jit(solution)/shard_map/psum | solution.py:14
  352.8 25.2 %all_gather.32 = bf16[32,2,4,768]{3,2,1,0:T(4,128)(2,1)S(1)} all-gather(bf16[4,2,4,768]{3,2,1,0:T(4,128)(2,1)S(1)} %get-tuple-element.11), channel_id=1, replica_groups=mesh['freq'=8,'sx'=16,'sy'=4] {'freq'}, dimensions={0}, use_global_device_ids=true | all-gather | bytes 442368 | tf_op jit(solution)/shard_map/all_gather | solution.py:78
  381.1 10.9 %all_to_all.34 = bf16[32,2,4,96]{3,2,1,0:T(4,128)(2,1)S(1)} all-to-all(bf16[32,2,4,96]{3,2,1,0:T(4,128)(2,1)S(1)} %copy.91), channel_id=1, replica_groups=mesh['freq'=8,'sx'=16,'sy'=4] {'freq'}, dimensions={0} | all-to-all | bytes 98304 | tf_op jit(solution)/shard_map/all_to_all | solution.py:89
  393.5 4.5 collective-permute-start.18
  400.0 2.4 collective-permute-start.16
  402.7 3.7 collective-permute-done.16
  406.8 8.6 %psum.120 = f32[4]{0:T(128)S(1)} all-reduce(f32[4]{0:T(128)S(1)} %multiply_reduce_fusion.2), channel_id=1, replica_groups=mesh['freq'=8,'sx'=16,'sy'=4] {'sy'}, use_global_device_ids=true, to_apply=%region_14.15 | all-reduce | flops 4 | bytes 32 | tf_op jit(solution)/shard_map/psum | solution.py:13
  415.4 23.5 %psum.121 = f32[4]{0:T(128)S(1)} all-reduce(f32[4]{0:T(128)S(1)} %psum.120), channel_id=1, replica_groups=mesh['freq'=8,'sx'=16,'sy'=4] {'sx'}, use_global_device_ids=true, to_apply=%region_15.16 | all-reduce | flops 4 | bytes 32 | tf_op jit(solution)/shard_map/psum | solution.py:14
  439.5 25.1 %all_gather.33 = bf16[32,2,4,768]{3,2,1,0:T(4,128)(2,1)S(1)} all-gather(bf16[4,2,4,768]{3,2,1,0:T(4,128)(2,1)S(1)} %get-tuple-element.9), channel_id=1, replica_groups=mesh['freq'=8,'sx'=16,'sy'=4] {'freq'}, dimensions={0}, use_global_device_ids=true | all-gather | bytes 442368 | tf_op jit(solution)/shard_map/all_gather | solution.py:78
  467.7 10.9 %all_to_all.35 = bf16[32,2,4,96]{3,2,1,0:T(4,128)(2,1)S(1)} all-to-all(bf16[32,2,4,96]{3,2,1,0:T(4,128)(2,1)S(1)} %copy.94), channel_id=1, replica_groups=mesh['freq'=8,'sx'=16,'sy'=4] {'freq'}, dimensions={0} | all-to-all | bytes 98304 | tf_op jit(solution)/shard_map/all_to_all | solution.py:89
  480.1 4.5 collective-permute-start.22
  486.6 2.4 collective-permute-start.20
  489.3 3.8 collective-permute-done.20
  493.4 8.9 %psum.122 = f32[4]{0:T(128)S(1)} all-reduce(f32[4]{0:T(128)S(1)} %multiply_reduce_fusion.1), channel_id=1, replica_groups=mesh['freq'=8,'sx'=16,'sy'=4] {'sy'}, use_global_device_ids=true, to_apply=%region_17.18 | all-reduce | flops 4 | bytes 32 | tf_op jit(solution)/shard_map/psum | solution.py:13
  502.2 23.5 %psum.123 = f32[4]{0:T(128)S(1)} all-reduce(f32[4]{0:T(128)S(1)} %psum.122), channel_id=1, replica_groups=mesh['freq'=8,'sx'=16,'sy'=4] {'sx'}, use_global_device_ids=true, to_apply=%region_18.19 | all-reduce | flops 4 | bytes 32 | tf_op jit(solution)/shard_map/psum | solution.py:14
  526.4 25.4 %all_gather.34 = bf16[32,2,4,768]{3,2,1,0:T(4,128)(2,1)S(1)} all-gather(bf16[4,2,4,768]{3,2,1,0:T(4,128)(2,1)S(1)} %subtract_convert_fusion), channel_id=1, replica_groups=mesh['freq'=8,'sx'=16,'sy'=4] {'freq'}, dimensions={0}, use_global_device_ids=true | all-gather | bytes 442368 | tf_op jit(solution)/shard_map/all_gather | solution.py:78
  554.8 10.9 %all_to_all.36 = bf16[32,2,4,96]{3,2,1,0:T(4,128)(2,1)S(1)} all-to-all(bf16[32,2,4,96]{3,2,1,0:T(4,128)(2,1)S(1)} %copy.97), channel_id=1, replica_groups=mesh['freq'=8,'sx'=16,'sy'=4] {'freq'}, dimensions={0} | all-to-all | bytes 98304 | tf_op jit(solution)/shard_map/all_to_all | solution.py:89
  567.3 4.5 collective-permute-start.26
  573.8 2.4 collective-permute-start.24
  576.4 3.8 collective-permute-done.24
  580.5 8.6 %psum.124 = f32[4]{0:T(128)S(1)} all-reduce(f32[4]{0:T(128)S(1)} %multiply_reduce_fusion), channel_id=1, replica_groups=mesh['freq'=8,'sx'=16,'sy'=4] {'sy'}, use_global_device_ids=true, to_apply=%region_20.21 | all-reduce | flops 4 | bytes 32 | tf_op jit(solution)/shard_map/psum | solution.py:13
  589.1 23.5 %psum.125 = f32[4]{0:T(128)S(1)} all-reduce(f32[4]{0:T(128)S(1)} %psum.124), channel_id=1, replica_groups=mesh['freq'=8,'sx'=16,'sy'=4] {'sx'}, use_global_device_ids=true, to_apply=%region_21.22 | all-reduce | flops 4 | bytes 32 | tf_op jit(solution)/shard_map/psum | solution.py:14
  613.3 25.2 %all_gather.35 = bf16[32,2,4,768]{3,2,1,0:T(4,128)(2,1)S(1)} all-gather(bf16[4,2,4,768]{3,2,1,0:T(4,128)(2,1)S(1)} %fusion.68), channel_id=1, replica_groups=mesh['freq'=8,'sx'=16,'sy'=4] {'freq'}, dimensions={0}, use_global_device_ids=true | all-gather | bytes 442368 | tf_op jit(solution)/shard_map/all_gather | solution.py:78
  642.3 3.4 all-to-all-start.7
  645.7 8.3 %all-to-all-done.7 = bf16[32,2,4,96]{3,2,1,0:T(4,128)(2,1)S(1)} async-done(((bf16[32,2,4,96]{3,2,1,0:T(4,128)(2,1)}), bf16[32,2,4,96]{3,2,1,0:T(4,128)(2,1)S(1)}, u32[]{:S(2)}, u32[]{:S(2)}) %all-to-all-start.7) | async-done | bytes 49184 | tf_op jit(solution)/shard_map/all_to_all | solution.py:89
  655.5 4.5 collective-permute-start.30
  662.0 2.4 collective-permute-start.28
  664.6 3.8 collective-permute-done.28
  668.7 8.9 %psum.126 = f32[4]{0:T(128)S(1)} all-reduce(f32[4]{0:T(128)S(1)} %fusion.65), channel_id=1, replica_groups=mesh['freq'=8,'sx'=16,'sy'=4] {'sy'}, use_global_device_ids=true, to_apply=%region_23.24 | all-reduce | flops 4 | bytes 32 | tf_op jit(solution)/shard_map/psum | solution.py:13
  678.3 23.6 %psum.127 = f32[4]{0:T(128)S(1)} all-reduce(f32[4]{0:T(128)S(1)} %psum.126), channel_id=1, replica_groups=mesh['freq'=8,'sx'=16,'sy'=4] {'sx'}, use_global_device_ids=true, to_apply=%region_24.25 | all-reduce | flops 4 | bytes 32 | tf_op jit(solution)/shard_map/psum | solution.py:14
  702.6 16.8 %scatter_custom_fusion = f32[1728]{0:T(1024)S(1)} fusion(s32[3072]{0:T(1024)S(1)} %reshape.442, f32[3072]{0:T(1024)S(1)} %reshape.444, f32[]{:T(128)} %constant.14.clone.1), kind=kCustom, calls=%fused_computation.212 | custom fusion | flops 3072 | bytes 6916 | tf_op jit(solution)/shard_map/scatter-add | solution.py:161
  719.4 15.0 %all-reduce.1 = f32[1728]{0:T(1024)S(1)} all-reduce(f32[1728]{0:T(1024)S(1)} %broadcast_multiply_fusion), channel_id=2, replica_groups=mesh['freq'=8,'sx'=16,'sy'=4] {'freq'}, use_global_device_ids=true, to_apply=%region_27.28.clone | all-reduce | flops 1728 | bytes 13824
  (278 shorter events, 64.3 us)
Async XLA Ops:
  46.6 68.7 %copy-start = (bf16[3072,96,4]{0,2,1:T(4,128)(2,1)S(1)}, bf16[3072,96,4]{0,2,1:T(4,128)(2,1)}, u32[]{:S(2)}) copy-start(bf16[3072,96,4]{0,2,1:T(4,128)(2,1)} %reshape_squeeze.7) | copy-start | bytes 7077892
  66.1 11.7 %all-to-all-start = ((bf16[32,2,4,96]{3,2,1,0:T(4,128)(2,1)}), bf16[32,2,4,96]{3,2,1,0:T(4,128)(2,1)S(1)}, u32[]{:S(2)}, u32[]{:S(2)}) async-start(bf16[32,2,4,96]{3,2,1,0:T(4,128)(2,1)} %copy.79), calls=%async_computation | async-start | bytes 131072 | tf_op jit(solution)/shard_map/all_to_all | solution.py:89
  78.0 10.2 %collective-permute-start.1 = (bf16[4,2,1,768]{3,2,1,0:T(2,128)(2,1)S(1)}, bf16[4,2,1,768]{3,2,1,0:T(2,128)(2,1)S(1)}, u32[]{:S(2)}, u32[]{:S(2)}) collective-permute-start(bf16[4,2,1,768]{3,2,1,0:T(2,128)(2,1)S(1)} %get-tuple-element.110), channel_id=1, source_target_pairs={{4,0},{8,4},{12,8},{16,12},{20,16},{24,20},{28,24},{32,28},{36,32}... | collective-permute-start | bytes 36872 | tf_op jit(solution)/shard_map/ppermute | solution.py:30
  79.9 8.3 %collective-permute-start = (bf16[4,2,1,768]{3,2,1,0:T(2,128)(2,1)S(1)}, bf16[4,2,1,768]{3,2,1,0:T(2,128)(2,1)S(1)}, u32[]{:S(2)}, u32[]{:S(2)}) collective-permute-start(bf16[4,2,1,768]{3,2,1,0:T(2,128)(2,1)S(1)} %get-tuple-element.107), channel_id=1, source_target_pairs={{0,4},{4,8},{8,12},{12,16},{16,20},{20,24},{24,28},{28,32},{32,36}... | collective-permute-start | bytes 36872 | tf_op jit(solution)/shard_map/ppermute | solution.py:28
  82.3 5.9 collective-permute-start.3
  83.6 6.1 collective-permute-start.2
  118.8 11.7 %all-to-all-start.1 = ((bf16[32,2,4,96]{3,2,1,0:T(4,128)(2,1)}), bf16[32,2,4,96]{3,2,1,0:T(4,128)(2,1)S(1)}, u32[]{:S(2)}, u32[]{:S(2)}) async-start(bf16[32,2,4,96]{3,2,1,0:T(4,128)(2,1)} %copy.82), calls=%async_computation.1 | async-start | bytes 131072 | tf_op jit(solution)/shard_map/all_to_all | solution.py:89
  130.7 10.7 %collective-permute-start.7 = (bf16[4,2,1,768]{3,2,1,0:T(2,128)(2,1)S(1)}, bf16[4,2,1,768]{3,2,1,0:T(2,128)(2,1)S(1)}, u32[]{:S(2)}, u32[]{:S(2)}) collective-permute-start(bf16[4,2,1,768]{3,2,1,0:T(2,128)(2,1)S(1)} %get-tuple-element.102), channel_id=1, source_target_pairs={{1,0},{2,1},{3,2},{5,4},{6,5},{7,6},{9,8},{10,9},{11,10},{13,12},{... | collective-permute-start | bytes 36872 | tf_op jit(solution)/shard_map/ppermute | solution.py:30
  132.0 9.4 %collective-permute-start.6 = (bf16[4,2,1,768]{3,2,1,0:T(2,128)(2,1)S(1)}, bf16[4,2,1,768]{3,2,1,0:T(2,128)(2,1)S(1)}, u32[]{:S(2)}, u32[]{:S(2)}) collective-permute-start(bf16[4,2,1,768]{3,2,1,0:T(2,128)(2,1)S(1)} %get-tuple-element.103), channel_id=1, source_target_pairs={{0,1},{1,2},{2,3},{4,5},{5,6},{6,7},{8,9},{9,10},{10,11},{12,13},{... | collective-permute-start | bytes 36872 | tf_op jit(solution)/shard_map/ppermute | solution.py:28
  137.1 4.5 collective-permute-start.5
  139.0 6.4 collective-permute-start.4
  218.6 10.2 %collective-permute-start.11 = (bf16[4,2,1,768]{3,2,1,0:T(2,128)(2,1)S(1)}, bf16[4,2,1,768]{3,2,1,0:T(2,128)(2,1)S(1)}, u32[]{:S(2)}, u32[]{:S(2)}) collective-permute-start(bf16[4,2,1,768]{3,2,1,0:T(2,128)(2,1)S(1)} %get-tuple-element.96), channel_id=1, source_target_pairs={{1,0},{2,1},{3,2},{5,4},{6,5},{7,6},{9,8},{10,9},{11,10},{13,12},{... | collective-permute-start | bytes 36872 | tf_op jit(solution)/shard_map/ppermute | solution.py:30
  219.9 9.0 %collective-permute-start.10 = (bf16[4,2,1,768]{3,2,1,0:T(2,128)(2,1)S(1)}, bf16[4,2,1,768]{3,2,1,0:T(2,128)(2,1)S(1)}, u32[]{:S(2)}, u32[]{:S(2)}) collective-permute-start(bf16[4,2,1,768]{3,2,1,0:T(2,128)(2,1)S(1)} %get-tuple-element.97), channel_id=1, source_target_pairs={{0,1},{1,2},{2,3},{4,5},{5,6},{6,7},{8,9},{9,10},{10,11},{12,13},{... | collective-permute-start | bytes 36872 | tf_op jit(solution)/shard_map/ppermute | solution.py:28
  224.5 4.5 collective-permute-start.9
  226.4 6.4 collective-permute-start.8
  229.0 36.7 %copy-start.9 = (f32[4,2,1,768]{3,2,1,0:T(1,128)}, f32[4,2,1,768]{3,2,1,0:T(1,128)S(1)}, u32[]{:S(2)}) copy-start(f32[4,2,1,768]{3,2,1,0:T(1,128)S(1)} %get-tuple-element.55) | copy-start | bytes 73732
  229.0 36.7 %copy-start.11 = (f32[4,2,1,768]{3,2,1,0:T(1,128)}, f32[4,2,1,768]{3,2,1,0:T(1,128)S(1)}, u32[]{:S(2)}) copy-start(f32[4,2,1,768]{3,2,1,0:T(1,128)S(1)} %get-tuple-element.56) | copy-start | bytes 73732
  232.9 32.8 %copy-start.13 = (f32[4,2,1,768]{3,2,1,0:T(1,128)}, f32[4,2,1,768]{3,2,1,0:T(1,128)S(1)}, u32[]{:S(2)}) copy-start(f32[4,2,1,768]{3,2,1,0:T(1,128)S(1)} %get-tuple-element.53) | copy-start | bytes 73732
  232.9 32.8 %copy-start.15 = (f32[4,2,1,768]{3,2,1,0:T(1,128)}, f32[4,2,1,768]{3,2,1,0:T(1,128)S(1)}, u32[]{:S(2)}) copy-start(f32[4,2,1,768]{3,2,1,0:T(1,128)S(1)} %get-tuple-element.54) | copy-start | bytes 73732
  265.5 39.4 %copy-start.41 = (f32[4]{0:T(128)}, f32[4]{0:T(128)S(1)}, u32[]{:S(2)}) copy-start(f32[4]{0:T(128)S(1)} %psum.117) | copy-start | bytes 52
  265.5 26.6 %copy-start.32 = (f32[4]{0:T(128)}, f32[4]{0:T(128)S(1)}, u32[]{:S(2)}) copy-start(f32[4]{0:T(128)S(1)} %div.25) | copy-start | bytes 52
  305.1 10.2 %collective-permute-start.15 = (bf16[4,2,1,768]{3,2,1,0:T(2,128)(2,1)S(1)}, bf16[4,2,1,768]{3,2,1,0:T(2,128)(2,1)S(1)}, u32[]{:S(2)}, u32[]{:S(2)}) collective-permute-start(bf16[4,2,1,768]{3,2,1,0:T(2,128)(2,1)S(1)} %get-tuple-element.90), channel_id=1, source_target_pairs={{1,0},{2,1},{3,2},{5,4},{6,5},{7,6},{9,8},{10,9},{11,10},{13,12},{... | collective-permute-start | bytes 36872 | tf_op jit(solution)/shard_map/ppermute | solution.py:30
  306.4 9.0 %collective-permute-start.14 = (bf16[4,2,1,768]{3,2,1,0:T(2,128)(2,1)S(1)}, bf16[4,2,1,768]{3,2,1,0:T(2,128)(2,1)S(1)}, u32[]{:S(2)}, u32[]{:S(2)}) collective-permute-start(bf16[4,2,1,768]{3,2,1,0:T(2,128)(2,1)S(1)} %get-tuple-element.91), channel_id=1, source_target_pairs={{0,1},{1,2},{2,3},{4,5},{5,6},{6,7},{8,9},{9,10},{10,11},{12,13},{... | collective-permute-start | bytes 36872 | tf_op jit(solution)/shard_map/ppermute | solution.py:28
  311.0 4.5 collective-permute-start.13
  312.9 6.4 collective-permute-start.12
  379.8 59.1 %copy-start.42 = (f32[4]{0:T(128)S(1)}, f32[4]{0:T(128)}, u32[]{:S(2)}) copy-start(f32[4]{0:T(128)} %copy-done.41) | copy-start | bytes 52
  392.2 10.2 %collective-permute-start.19 = (bf16[4,2,1,768]{3,2,1,0:T(2,128)(2,1)S(1)}, bf16[4,2,1,768]{3,2,1,0:T(2,128)(2,1)S(1)}, u32[]{:S(2)}, u32[]{:S(2)}) collective-permute-start(bf16[4,2,1,768]{3,2,1,0:T(2,128)(2,1)S(1)} %get-tuple-element.84), channel_id=1, source_target_pairs={{1,0},{2,1},{3,2},{5,4},{6,5},{7,6},{9,8},{10,9},{11,10},{13,12},{... | collective-permute-start | bytes 36872 | tf_op jit(solution)/shard_map/ppermute | solution.py:30
  393.5 9.0 %collective-permute-start.18 = (bf16[4,2,1,768]{3,2,1,0:T(2,128)(2,1)S(1)}, bf16[4,2,1,768]{3,2,1,0:T(2,128)(2,1)S(1)}, u32[]{:S(2)}, u32[]{:S(2)}) collective-permute-start(bf16[4,2,1,768]{3,2,1,0:T(2,128)(2,1)S(1)} %get-tuple-element.85), channel_id=1, source_target_pairs={{0,1},{1,2},{2,3},{4,5},{5,6},{6,7},{8,9},{9,10},{10,11},{12,13},{... | collective-permute-start | bytes 36872 | tf_op jit(solution)/shard_map/ppermute | solution.py:28
  398.1 4.5 collective-permute-start.17
  400.0 6.4 collective-permute-start.16
  402.6 36.4 %copy-start.17 = (f32[4,2,1,768]{3,2,1,0:T(1,128)}, f32[4,2,1,768]{3,2,1,0:T(1,128)S(1)}, u32[]{:S(2)}) copy-start(f32[4,2,1,768]{3,2,1,0:T(1,128)S(1)} %get-tuple-element.47) | copy-start | bytes 73732
  402.6 36.4 %copy-start.19 = (f32[4,2,1,768]{3,2,1,0:T(1,128)}, f32[4,2,1,768]{3,2,1,0:T(1,128)S(1)}, u32[]{:S(2)}) copy-start(f32[4,2,1,768]{3,2,1,0:T(1,128)S(1)} %get-tuple-element.48) | copy-start | bytes 73732
  406.6 32.5 %copy-start.21 = (f32[4,2,1,768]{3,2,1,0:T(1,128)}, f32[4,2,1,768]{3,2,1,0:T(1,128)S(1)}, u32[]{:S(2)}) copy-start(f32[4,2,1,768]{3,2,1,0:T(1,128)S(1)} %get-tuple-element.45) | copy-start | bytes 73732
  406.6 32.5 %copy-start.23 = (f32[4,2,1,768]{3,2,1,0:T(1,128)}, f32[4,2,1,768]{3,2,1,0:T(1,128)S(1)}, u32[]{:S(2)}) copy-start(f32[4,2,1,768]{3,2,1,0:T(1,128)S(1)} %get-tuple-element.46) | copy-start | bytes 73732
  466.4 59.3 %copy-start.44 = (f32[4]{0:T(128)S(1)}, f32[4]{0:T(128)}, u32[]{:S(2)}) copy-start(f32[4]{0:T(128)} %copy-done.43) | copy-start | bytes 52
  478.8 10.2 %collective-permute-start.23 = (bf16[4,2,1,768]{3,2,1,0:T(2,128)(2,1)S(1)}, bf16[4,2,1,768]{3,2,1,0:T(2,128)(2,1)S(1)}, u32[]{:S(2)}, u32[]{:S(2)}) collective-permute-start(bf16[4,2,1,768]{3,2,1,0:T(2,128)(2,1)S(1)} %get-tuple-element.78), channel_id=1, source_target_pairs={{1,0},{2,1},{3,2},{5,4},{6,5},{7,6},{9,8},{10,9},{11,10},{13,12},{... | collective-permute-start | bytes 36872 | tf_op jit(solution)/shard_map/ppermute | solution.py:30
  480.1 9.0 %collective-permute-start.22 = (bf16[4,2,1,768]{3,2,1,0:T(2,128)(2,1)S(1)}, bf16[4,2,1,768]{3,2,1,0:T(2,128)(2,1)S(1)}, u32[]{:S(2)}, u32[]{:S(2)}) collective-permute-start(bf16[4,2,1,768]{3,2,1,0:T(2,128)(2,1)S(1)} %get-tuple-element.79), channel_id=1, source_target_pairs={{0,1},{1,2},{2,3},{4,5},{5,6},{6,7},{8,9},{9,10},{10,11},{12,13},{... | collective-permute-start | bytes 36872 | tf_op jit(solution)/shard_map/ppermute | solution.py:28
  484.7 4.5 collective-permute-start.21
  486.6 6.4 collective-permute-start.20
  553.6 59.1 %copy-start.45 = (f32[4]{0:T(128)S(1)}, f32[4]{0:T(128)}, u32[]{:S(2)}) copy-start(f32[4]{0:T(128)} %copy-done.43) | copy-start | bytes 52
  566.0 10.2 %collective-permute-start.27 = (bf16[4,2,1,768]{3,2,1,0:T(2,128)(2,1)S(1)}, bf16[4,2,1,768]{3,2,1,0:T(2,128)(2,1)S(1)}, u32[]{:S(2)}, u32[]{:S(2)}) collective-permute-start(bf16[4,2,1,768]{3,2,1,0:T(2,128)(2,1)S(1)} %get-tuple-element.72), channel_id=1, source_target_pairs={{1,0},{2,1},{3,2},{5,4},{6,5},{7,6},{9,8},{10,9},{11,10},{13,12},{... | collective-permute-start | bytes 36872 | tf_op jit(solution)/shard_map/ppermute | solution.py:30
  567.3 9.0 %collective-permute-start.26 = (bf16[4,2,1,768]{3,2,1,0:T(2,128)(2,1)S(1)}, bf16[4,2,1,768]{3,2,1,0:T(2,128)(2,1)S(1)}, u32[]{:S(2)}, u32[]{:S(2)}) collective-permute-start(bf16[4,2,1,768]{3,2,1,0:T(2,128)(2,1)S(1)} %get-tuple-element.73), channel_id=1, source_target_pairs={{0,1},{1,2},{2,3},{4,5},{5,6},{6,7},{8,9},{9,10},{10,11},{12,13},{... | collective-permute-start | bytes 36872 | tf_op jit(solution)/shard_map/ppermute | solution.py:28
  571.9 4.5 collective-permute-start.25
  573.8 6.4 collective-permute-start.24
  640.3 5.4 copy-start.26
  640.3 28.4 %copy-start.27 = (s32[1,1,4,768]{3,2,1,0:T(4,128)S(1)}, s32[1,1,4,768]{3,2,1,0:T(4,128)}, u32[]{:S(2)}) copy-start(s32[1,1,4,768]{3,2,1,0:T(4,128)} %param.13) | copy-start | bytes 36868
  640.3 61.5 %copy-start.38 = (f32[4]{0:T(128)S(1)}, f32[4]{0:T(128)}, u32[]{:S(2)}) copy-start(f32[4]{0:T(128)} %copy-done.37) | copy-start | bytes 52
  640.3 62.0 %copy-start.29 = (f32[4]{0:T(128)S(1)}, f32[4]{0:T(128)}, u32[]{:S(2)}) copy-start(f32[4]{0:T(128)} %copy-done.28) | copy-start | bytes 52
  640.3 62.0 %copy-start.31 = (f32[4]{0:T(128)S(1)}, f32[4]{0:T(128)}, u32[]{:S(2)}) copy-start(f32[4]{0:T(128)} %copy-done.30) | copy-start | bytes 52
  641.4 93.7 %copy-start.10 = (f32[4,2,1,768]{3,2,1,0:T(1,128)S(1)}, f32[4,2,1,768]{3,2,1,0:T(1,128)}, u32[]{:S(2)}) copy-start(f32[4,2,1,768]{3,2,1,0:T(1,128)} %copy-done.9) | copy-start | bytes 73732
  641.4 93.7 %copy-start.12 = (f32[4,2,1,768]{3,2,1,0:T(1,128)S(1)}, f32[4,2,1,768]{3,2,1,0:T(1,128)}, u32[]{:S(2)}) copy-start(f32[4,2,1,768]{3,2,1,0:T(1,128)} %copy-done.11) | copy-start | bytes 73732
  641.4 93.6 %copy-start.14 = (f32[4,2,1,768]{3,2,1,0:T(1,128)S(1)}, f32[4,2,1,768]{3,2,1,0:T(1,128)}, u32[]{:S(2)}) copy-start(f32[4,2,1,768]{3,2,1,0:T(1,128)} %copy-done.13) | copy-start | bytes 73732
  641.4 93.6 %copy-start.16 = (f32[4,2,1,768]{3,2,1,0:T(1,128)S(1)}, f32[4,2,1,768]{3,2,1,0:T(1,128)}, u32[]{:S(2)}) copy-start(f32[4,2,1,768]{3,2,1,0:T(1,128)} %copy-done.15) | copy-start | bytes 73732
  641.4 93.6 %copy-start.18 = (f32[4,2,1,768]{3,2,1,0:T(1,128)S(1)}, f32[4,2,1,768]{3,2,1,0:T(1,128)}, u32[]{:S(2)}) copy-start(f32[4,2,1,768]{3,2,1,0:T(1,128)} %copy-done.17) | copy-start | bytes 73732
  641.4 93.6 %copy-start.20 = (f32[4,2,1,768]{3,2,1,0:T(1,128)S(1)}, f32[4,2,1,768]{3,2,1,0:T(1,128)}, u32[]{:S(2)}) copy-start(f32[4,2,1,768]{3,2,1,0:T(1,128)} %copy-done.19) | copy-start | bytes 73732
  641.5 93.6 %copy-start.22 = (f32[4,2,1,768]{3,2,1,0:T(1,128)S(1)}, f32[4,2,1,768]{3,2,1,0:T(1,128)}, u32[]{:S(2)}) copy-start(f32[4,2,1,768]{3,2,1,0:T(1,128)} %copy-done.21) | copy-start | bytes 73732
  641.5 93.6 %copy-start.24 = (f32[4,2,1,768]{3,2,1,0:T(1,128)S(1)}, f32[4,2,1,768]{3,2,1,0:T(1,128)}, u32[]{:S(2)}) copy-start(f32[4,2,1,768]{3,2,1,0:T(1,128)} %copy-done.23) | copy-start | bytes 73732
  641.5 93.6 %copy-start.33 = (f32[4]{0:T(128)S(1)}, f32[4]{0:T(128)}, u32[]{:S(2)}) copy-start(f32[4]{0:T(128)} %copy-done.32) | copy-start | bytes 52
  641.5 93.6 %copy-start.35 = (f32[4]{0:T(128)S(1)}, f32[4]{0:T(128)}, u32[]{:S(2)}) copy-start(f32[4]{0:T(128)} %copy-done.34) | copy-start | bytes 52
  642.3 11.7 %all-to-all-start.7 = ((bf16[32,2,4,96]{3,2,1,0:T(4,128)(2,1)}), bf16[32,2,4,96]{3,2,1,0:T(4,128)(2,1)S(1)}, u32[]{:S(2)}, u32[]{:S(2)}) async-start(bf16[32,2,4,96]{3,2,1,0:T(4,128)(2,1)} %copy.100), calls=%async_computation.7 | async-start | bytes 131072 | tf_op jit(solution)/shard_map/all_to_all | solution.py:89
  654.2 10.2 %collective-permute-start.31 = (bf16[4,2,1,768]{3,2,1,0:T(2,128)(2,1)S(1)}, bf16[4,2,1,768]{3,2,1,0:T(2,128)(2,1)S(1)}, u32[]{:S(2)}, u32[]{:S(2)}) collective-permute-start(bf16[4,2,1,768]{3,2,1,0:T(2,128)(2,1)S(1)} %get-tuple-element.66), channel_id=1, source_target_pairs={{1,0},{2,1},{3,2},{5,4},{6,5},{7,6},{9,8},{10,9},{11,10},{13,12},{... | collective-permute-start | bytes 36872 | tf_op jit(solution)/shard_map/ppermute | solution.py:30
  655.5 9.0 %collective-permute-start.30 = (bf16[4,2,1,768]{3,2,1,0:T(2,128)(2,1)S(1)}, bf16[4,2,1,768]{3,2,1,0:T(2,128)(2,1)S(1)}, u32[]{:S(2)}, u32[]{:S(2)}) collective-permute-start(bf16[4,2,1,768]{3,2,1,0:T(2,128)(2,1)S(1)} %get-tuple-element.67), channel_id=1, source_target_pairs={{0,1},{1,2},{2,3},{4,5},{5,6},{6,7},{8,9},{9,10},{10,11},{12,13},{... | collective-permute-start | bytes 36872 | tf_op jit(solution)/shard_map/ppermute | solution.py:28
  660.1 4.5 collective-permute-start.29
  662.0 6.4 collective-permute-start.28
  (17 other events, 23.0 us)
